TPU v7x, 256 devices: a whole 4x4x8 slice. The times are simulated.
256 devices in a mesh: expert: 16 (over y, x), hidden: 16 (over z, core).
Axes of the slice: x: 4, y: 4, z: 8, core: 2. Of those that a mesh axis runs over, the one named last changes fastest.
Arguments:
- layer_input: bfloat16 [4096, 4096], P('expert', 'hidden'), may hold values from -6 to 6
- output_grad: bfloat16 [4096, 4096], P('expert', 'hidden'), may hold values from -1.5 to 1.5
- latent_saved: bfloat16 [4096, 1024], P('expert'), may hold values from -6 to 6
- combined_saved: bfloat16 [4096, 1024], P('expert'), may hold values from -6 to 6
- expert_ids: int32 [4096, 22], P('expert'), may hold values from 0 to 511, as said below
- gate_values: bfloat16 [4096, 22], P('expert'), may hold values from 0.099609375 to 1.5
- down_proj: bfloat16 [1024, 4096], P(None, 'hidden'), may hold values from -0.09375 to 0.09375
- up_proj: bfloat16 [1024, 4096], P(None, 'hidden'), may hold values from -0.1875 to 0.1875
- expert_in: bfloat16 [16, 1024, 2688], P('expert', None, 'hidden'), may hold values from -0.1875 to 0.1875
- expert_out: bfloat16 [16, 2688, 1024], P('expert', 'hidden'), may hold values from -0.125 to 0.125
Outputs:
- input_grad: bfloat16 [4096, 4096], P('expert', 'hidden')
- down_grad: float32 [1024, 4096], P('expert', 'hidden')
- up_grad: float32 [1024, 4096], P('expert', 'hidden')
- gate_grad: float32 [4096, 22], P('expert')
- expert_in_grad: float32 [16, 1024, 2688], P('expert', None, 'hidden')
- expert_out_grad: float32 [16, 2688, 1024], P('expert', 'hidden')
Inputs may be any that keep to these rules, and one draw needn't show every extreme that they name: `expert_ids`: each row names 22 different experts. In each aligned block of 256 rows (the rows of one index of the expert axis) each expert below 16 is named by at most 24 rows; some expert below 16 is named by exactly 24 rows in every block.
All inputs are finite; a program needn't handle non-finite values.
Results may differ from a plain program's by a relative error of at most 0.0065.
Values may be sent and summed in bfloat16 or wider, within the bound.
No kernel may reach another device: no remote copies, remote signals or barrier semaphores. Data moves between devices by JAX's collectives and lax.ppermute only.
A program may use at most 64 MiB of HBM per device.

v0:
```python
import jax
import jax.numpy as jnp
from jax import lax
from jax.sharding import PartitionSpec as P


def slot_layout(table, groups, local_count):
    tokens_here = table.shape[0]
    return table.T.reshape(groups, local_count, tokens_here).transpose(1, 0, 2)[:, :, None, :]


def on_device(
    layer_input,
    output_grad,
    latent_saved,
    combined_saved,
    expert_ids,
    gate_values,
    down_proj,
    up_proj,
    expert_in,
    expert_out,
):
    groups = lax.axis_size("expert")
    tokens_here = layer_input.shape[0]
    latent_width = latent_saved.shape[1]
    local_count = expert_in.shape[0]
    capacity = tokens_here * 3 // 32
    live_count = local_count * groups
    slot_total = local_count * groups * capacity
    partial_cot = jnp.einsum("td,ld->tl", output_grad, up_proj, preferred_element_type=jnp.float32)
    member = expert_ids[:, :, None] == jnp.arange(live_count, dtype=jnp.int32)[None, None, :]
    per_token = jnp.sum(member.astype(jnp.int32), axis=1)
    before = jnp.cumsum(per_token, axis=0) - per_token
    gate_token = jnp.sum(
        jnp.where(member, gate_values.astype(jnp.float32)[:, :, None], 0.0), axis=1
    )
    rank_iota = jnp.arange(capacity, dtype=jnp.int32)[None, None, :, None]
    hit_slot = (slot_layout(per_token, groups, local_count) == 1) & (
        slot_layout(before, groups, local_count) == rank_iota
    )
    gate_slot = jnp.sum(
        jnp.where(hit_slot, slot_layout(gate_token, groups, local_count), 0.0), axis=3
    )
    gate_send = gate_slot.astype(jnp.bfloat16)
    dispatch_bf = hit_slot.astype(jnp.bfloat16).reshape(slot_total, tokens_here)
    cot_full = lax.psum(partial_cot, "hidden")
    cot_rows = jnp.dot(
        dispatch_bf, cot_full.astype(jnp.bfloat16), preferred_element_type=jnp.float32
    ).astype(jnp.bfloat16)
    latent_rows = jnp.dot(dispatch_bf, latent_saved, preferred_element_type=jnp.float32).astype(
        jnp.bfloat16
    )
    cot_recv, latent_recv, gate_recv = (
        lax.all_to_all(
            cot_rows.reshape(local_count, groups, capacity, latent_width),
            "expert",
            split_axis=1,
            concat_axis=1,
            tiled=True,
        ),
        lax.all_to_all(
            latent_rows.reshape(local_count, groups, capacity, latent_width),
            "expert",
            split_axis=1,
            concat_axis=1,
            tiled=True,
        ),
        lax.all_to_all(gate_send, "expert", split_axis=1, concat_axis=1, tiled=True),
    )
    row_count = groups * capacity
    cot_block = cot_recv.reshape(local_count, row_count, latent_width)
    latent_block = latent_recv.reshape(local_count, row_count, latent_width)
    gate_block = gate_recv.reshape(local_count, row_count).astype(jnp.float32)
    pre_act = jnp.einsum(
        "erl,elf->erf", latent_block, expert_in, preferred_element_type=jnp.float32
    )
    relu_out = jnp.maximum(pre_act, 0.0)
    back_proj = jnp.einsum(
        "erl,efl->erf", cot_block, expert_out, preferred_element_type=jnp.float32
    )
    gate_part = jnp.sum(back_proj * relu_out * relu_out, axis=2)
    scaled_act = (gate_block[:, :, None] * relu_out * relu_out).astype(jnp.bfloat16)
    pre_grad = (2.0 * gate_block[:, :, None] * relu_out * back_proj).astype(jnp.bfloat16)
    expert_out_grad = jnp.einsum(
        "erf,erl->efl", scaled_act, cot_block, preferred_element_type=jnp.float32
    )
    expert_in_grad = jnp.einsum(
        "erl,erf->elf", latent_block, pre_grad, preferred_element_type=jnp.float32
    )
    latent_back = jnp.einsum(
        "erf,elf->erl", pre_grad, expert_in, preferred_element_type=jnp.float32
    )
    latent_back = latent_back.reshape(local_count, groups, capacity, latent_width)
    gate_part = gate_part.reshape(local_count, groups, capacity)
    dispatch_full = hit_slot.astype(jnp.float32)
    dispatch_flat = dispatch_full.reshape(slot_total, tokens_here)
    rows_home, gate_home = (
        lax.all_to_all(latent_back, "expert", split_axis=1, concat_axis=1, tiled=True),
        lax.all_to_all(gate_part, "expert", split_axis=1, concat_axis=1, tiled=True),
    )
    token_sums = jnp.dot(
        dispatch_flat.T,
        rows_home.reshape(slot_total, latent_width),
        precision=lax.Precision.HIGHEST,
        preferred_element_type=jnp.float32,
    )
    by_expert = jnp.sum(dispatch_full * gate_home[:, :, :, None], axis=2)
    by_expert = by_expert.transpose(2, 1, 0).reshape(tokens_here, live_count)
    gate_local = jnp.sum(jnp.where(member, by_expert[:, None, :], 0.0), axis=2)
    latent_grad, gate_grad = lax.psum((token_sums, gate_local), "hidden")
    latent_bf = latent_grad.astype(jnp.bfloat16)
    input_grad = jnp.dot(latent_bf, down_proj, preferred_element_type=jnp.float32).astype(
        jnp.bfloat16
    )
    down_term = jnp.einsum("tl,td->ld", latent_bf, layer_input, preferred_element_type=jnp.float32)
    up_term = jnp.einsum(
        "tl,td->ld", combined_saved, output_grad, preferred_element_type=jnp.float32
    )
    down_grad, up_grad = (
        lax.psum_scatter(down_term, "expert", scatter_dimension=0, tiled=True),
        lax.psum_scatter(up_term, "expert", scatter_dimension=0, tiled=True),
    )
    return (input_grad, down_grad, up_grad, gate_grad, expert_in_grad, expert_out_grad)


def solution(mesh):
    return jax.shard_map(
        on_device,
        mesh=mesh,
        in_specs=(
            P("expert", "hidden"),
            P("expert", "hidden"),
            P("expert", None),
            P("expert", None),
            P("expert", None),
            P("expert", None),
            P(None, "hidden"),
            P(None, "hidden"),
            P("expert", None, "hidden"),
            P("expert", "hidden", None),
        ),
        out_specs=(
            P("expert", "hidden"),
            P("expert", "hidden"),
            P("expert", "hidden"),
            P("expert", None),
            P("expert", None, "hidden"),
            P("expert", "hidden", None),
        ),
        check_vma=False,
    )
```

profile of v0, /device:TPU:2, one launch (start us, length us, event | category | flops | bytes accessed | tf_op | source)
XLA Modules:
  0.0 312.9 jit_solution(7600036610667485425)
XLA Ops:
  7.2 0.0 copy-start
  7.2 0.8 convert_reduce_fusion
  8.1 0.1 eq.79
  8.1 0.6 reduce-window.6
  8.7 0.2 slice_reduce_fusion
  9.0 0.1 bitcast_subtract_fusion
  9.0 1.5 fusion.23
  10.5 62.0 %all-reduce.3 = bf16[256,1024]{1,0:T(8,128)(2,1)S(1)} all-reduce(f32[256,1024]{1,0:T(8,128)S(1)} %fusion.23), channel_id=1, replica_groups=mesh['expert'=16,'hidden'=16] {'hidden'}, use_global_device_ids=true, to_apply=%region_5.6 | all-reduce | flops 262144 | bytes 1572864 | tf_op jit(solution)/shard_map/psum | solution.py:47
  72.5 0.1 fusion.9
  72.7 1.3 convolution_convert_fusion
  73.9 7.5 %all-to-all-start.2 = ((bf16[1,16,24,1024]{3,2,0,1:T(8,128)(2,1)}), bf16[1,16,24,1024]{3,2,0,1:T(8,128)(2,1)S(1)}, u32[]{:S(2)}, u32[]{:S(2)}) async-start(bf16[1,16,24,1024]{3,2,0,1:T(8,128)(2,1)} %bitcast.11), calls=%async_computation.2 | async-start | bytes 1572864 | tf_op jit(solution)/shard_map/all_to_all | solution.py:55
  81.4 0.0 copy-done
  81.4 0.0 copy-start.5
  81.4 1.3 convolution_convert_fusion.1
  82.7 8.9 %all-to-all-done.2 = bf16[1,16,24,1024]{3,2,0,1:T(8,128)(2,1)S(1)} async-done(((bf16[1,16,24,1024]{3,2,0,1:T(8,128)(2,1)}), bf16[1,16,24,1024]{3,2,0,1:T(8,128)(2,1)S(1)}, u32[]{:S(2)}, u32[]{:S(2)}) %all-to-all-start.2) | async-done | bytes 786464 | tf_op jit(solution)/shard_map/all_to_all | solution.py:55
  91.6 4.9 %all-to-all-start.1 = ((bf16[1,16,24,1024]{3,2,0,1:T(8,128)(2,1)}), bf16[1,16,24,1024]{3,2,0,1:T(8,128)(2,1)S(1)}, u32[]{:S(2)}, u32[]{:S(2)}) async-start(bf16[1,16,24,1024]{3,2,0,1:T(8,128)(2,1)} %bitcast.7), calls=%async_computation.1 | async-start | bytes 1572864 | tf_op jit(solution)/shard_map/all_to_all | solution.py:62
  96.5 0.0 copy-done.5
  96.5 0.0 copy-start.7
  96.5 0.4 fusion.11
  96.9 9.9 %all-to-all-done.1 = bf16[1,16,24,1024]{3,2,0,1:T(8,128)(2,1)S(1)} async-done(((bf16[1,16,24,1024]{3,2,0,1:T(8,128)(2,1)}), bf16[1,16,24,1024]{3,2,0,1:T(8,128)(2,1)S(1)}, u32[]{:S(2)}, u32[]{:S(2)}) %all-to-all-start.1) | async-done | bytes 786464 | tf_op jit(solution)/shard_map/all_to_all | solution.py:62
  106.8 0.4 fusion.17
  107.2 0.7 reshape.184
  107.9 4.7 %all-to-all-start.4 = ((f32[1,16,24]{2,0,1:T(1,128)}), f32[1,16,24]{2,0,1:T(1,128)S(1)}, u32[]{:S(2)}, u32[]{:S(2)}) async-start(f32[1,16,24]{2,0,1:T(1,128)} %reshape.184), calls=%async_computation.6 | async-start | bytes 16384 | tf_op jit(solution)/shard_map/all_to_all | solution.py:100
  112.7 6.2 %all-to-all-done.4 = f32[1,16,24]{2,0,1:T(1,128)S(1)} async-done(((f32[1,16,24]{2,0,1:T(1,128)}), f32[1,16,24]{2,0,1:T(1,128)S(1)}, u32[]{:S(2)}, u32[]{:S(2)}) %all-to-all-start.4) | async-done | bytes 1568 | tf_op jit(solution)/shard_map/all_to_all | solution.py:100
  118.9 0.2 select_reduce_fusion
  119.0 0.1 select_reduce_fusion.2
  119.2 0.2 select_reduce_fusion.1
  119.4 10.6 %all_to_all.25 = bf16[1,16,24]{2,0,1:T(2,128)(2,1)S(1)} all-to-all(bf16[1,16,24]{2,0,1:T(2,128)(2,1)S(1)} %copy.45), channel_id=1, replica_groups=mesh['expert'=16,'hidden'=16] {'expert'}, dimensions={1} | all-to-all | bytes 1536 | tf_op jit(solution)/shard_map/all_to_all | solution.py:69
  130.0 0.1 reshape.185
  130.1 0.1 copy.48
  130.3 1.5 convolution_bitcast_fusion
  131.8 5.7 %all-to-all-start.3 = ((f32[1,16,24,1024]{3,2,0,1:T(8,128)}), f32[1,16,24,1024]{3,2,0,1:T(8,128)}, u32[]{:S(2)}, u32[]{:S(2)}) async-start(f32[1,16,24,1024]{3,2,0,1:T(8,128)} %convolution_bitcast_fusion), calls=%async_computation.3 | async-start | bytes 3145728 | tf_op jit(solution)/shard_map/all_to_all | solution.py:99
  137.5 0.0 reduce-scatter.5.cloned.1.call-start
  137.6 1.3 fusion.24
  138.9 0.0 reduce-scatter.5.cloned.1.call-update
  138.9 0.0 copy-start.6
  138.9 0.0 reduce-scatter.3.cloned.1.call-start
  139.0 13.1 %all-to-all-done.3 = f32[1,16,24,1024]{3,2,0,1:T(8,128)} async-done(((f32[1,16,24,1024]{3,2,0,1:T(8,128)}), f32[1,16,24,1024]{3,2,0,1:T(8,128)}, u32[]{:S(2)}, u32[]{:S(2)}) %all-to-all-start.3) | async-done | bytes 1572896 | tf_op jit(solution)/shard_map/all_to_all | solution.py:99
  152.1 3.5 %fusion.2 = f32[256,1024]{1,0:T(8,128)} fusion(f32[1,16,24,1024]{3,2,0,1:T(8,128)} %all-to-all-done.3, s32[16,256]{1,0:T(8,128)S(1)} %bitcast_subtract_fusion, pred[16,256]{1,0:T(8,128)(4,1)S(1)} %bitcast_compare_fusion.1), kind=kOutput, calls=%fused_computation.5 | convolution fusion | flops 1208156160 | bytes 2641920 | tf_op jit(solution)/shard_map/dot_general | solution.py:102
  155.7 66.5 %all-reduce.4 = (bf16[256,1024]{1,0:T(8,128)(2,1)S(1)}, f32[256,22]{0,1:T(8,128)}) all-reduce(f32[256,1024]{1,0:T(8,128)} %fusion.2, f32[256,22]{0,1:T(8,128)S(1)} %get-tuple-element.6), channel_id=1, replica_groups=mesh['expert'=16,'hidden'=16] {'hidden'}, use_global_device_ids=true, to_apply=%region_6.7 | all-reduce | flops 267776 | bytes 1617920 | tf_op jit(solution)/shard_map/psum | solution.py:111
  222.1 1.3 fusion.25
  223.5 0.0 reduce-scatter.3.cloned.1.call-update
  223.5 0.0 copy-start.3
  223.5 1.2 convolution_bitcast_fusion.2
  224.7 1.2 convolution_bitcast_fusion.1
  225.9 0.0 copy-done.3
  225.9 1.0 convolution_convert_fusion.2
  226.9 79.2 %reduce-scatter.3.cloned.1.call-done = f32[64,256]{1,0:T(8,128)} async-done(((f32[1024,256]{1,0:T(8,128)}), f32[64,256]{1,0:T(8,128)}) %reduce-scatter.3.cloned.1.call-update) | async-done | bytes 65552 | tf_op jit(solution)/shard_map/reduce_scatter | solution.py:121
  (21 shorter events, 0.2 us)
Async XLA Ops:
  7.2 74.3 %copy-start = (bf16[256,1024]{1,0:T(8,128)(2,1)S(1)}, bf16[256,1024]{1,0:T(8,128)(2,1)}, u32[]{:S(2)}) copy-start(bf16[256,1024]{1,0:T(8,128)(2,1)} %param.12) | copy-start | bytes 1572868
  73.9 17.7 %all-to-all-start.2 = ((bf16[1,16,24,1024]{3,2,0,1:T(8,128)(2,1)}), bf16[1,16,24,1024]{3,2,0,1:T(8,128)(2,1)S(1)}, u32[]{:S(2)}, u32[]{:S(2)}) async-start(bf16[1,16,24,1024]{3,2,0,1:T(8,128)(2,1)} %bitcast.11), calls=%async_computation.2 | async-start | bytes 1572864 | tf_op jit(solution)/shard_map/all_to_all | solution.py:55
  81.4 15.1 %copy-start.5 = (bf16[1,168,1024]{2,1,0:T(8,128)(2,1)S(1)}, bf16[1,168,1024]{2,1,0:T(8,128)(2,1)}, u32[]{:S(2)}) copy-start(bf16[1,168,1024]{2,1,0:T(8,128)(2,1)} %param.19) | copy-start | bytes 1032196
  82.7 24.0 %copy-start.1 = (bf16[1,1024,168]{1,2,0:T(8,128)(2,1)S(1)}, bf16[1,1024,168]{1,2,0:T(8,128)(2,1)}, u32[]{:S(2)}) copy-start(bf16[1,1024,168]{1,2,0:T(8,128)(2,1)} %param.18) | copy-start | bytes 1032196
  91.6 15.2 %all-to-all-start.1 = ((bf16[1,16,24,1024]{3,2,0,1:T(8,128)(2,1)}), bf16[1,16,24,1024]{3,2,0,1:T(8,128)(2,1)S(1)}, u32[]{:S(2)}, u32[]{:S(2)}) async-start(bf16[1,16,24,1024]{3,2,0,1:T(8,128)(2,1)} %bitcast.7), calls=%async_computation.1 | async-start | bytes 1572864 | tf_op jit(solution)/shard_map/all_to_all | solution.py:62
  96.5 16.2 %copy-start.8 = (bf16[256,22]{0,1:T(8,128)(2,1)S(1)}, bf16[256,22]{0,1:T(8,128)(2,1)}, u32[]{:S(2)}) copy-start(bf16[256,22]{0,1:T(8,128)(2,1)} %param.15) | copy-start | bytes 33796
  96.5 22.5 %copy-start.7 = (s32[256,22]{0,1:T(8,128)S(1)}, s32[256,22]{0,1:T(8,128)}, u32[]{:S(2)}) copy-start(s32[256,22]{0,1:T(8,128)} %param.14) | copy-start | bytes 67588
  107.9 10.9 %all-to-all-start.4 = ((f32[1,16,24]{2,0,1:T(1,128)}), f32[1,16,24]{2,0,1:T(1,128)S(1)}, u32[]{:S(2)}, u32[]{:S(2)}) async-start(f32[1,16,24]{2,0,1:T(1,128)} %reshape.184), calls=%async_computation.6 | async-start | bytes 16384 | tf_op jit(solution)/shard_map/all_to_all | solution.py:100
  131.8 5.8 %copy-start.2 = (bf16[256,1024]{1,0:T(8,128)(2,1)S(1)}, bf16[256,1024]{1,0:T(8,128)(2,1)}, u32[]{:S(2)}) copy-start(bf16[256,1024]{1,0:T(8,128)(2,1)} %param.13) | copy-start | bytes 1572868
  131.8 5.8 %copy-start.4 = (bf16[256,256]{1,0:T(8,128)(2,1)S(1)}, bf16[256,256]{1,0:T(8,128)(2,1)}, u32[]{:S(2)}) copy-start(bf16[256,256]{1,0:T(8,128)(2,1)} %param.11) | copy-start | bytes 393220
  131.8 20.3 %all-to-all-start.3 = ((f32[1,16,24,1024]{3,2,0,1:T(8,128)}), f32[1,16,24,1024]{3,2,0,1:T(8,128)}, u32[]{:S(2)}, u32[]{:S(2)}) async-start(f32[1,16,24,1024]{3,2,0,1:T(8,128)} %convolution_bitcast_fusion), calls=%async_computation.3 | async-start | bytes 3145728 | tf_op jit(solution)/shard_map/all_to_all | solution.py:99
  137.5 89.4 %reduce-scatter.5.cloned.1.call-start = ((), (), s32[]{:S(2)}) async-start(), calls=%async_computation.8 | async-start | bytes 1114112 | tf_op jit(solution)/shard_map/reduce_scatter | solution.py:122
  138.9 83.2 %copy-start.6 = (bf16[256,256]{1,0:T(8,128)(2,1)S(1)}, bf16[256,256]{1,0:T(8,128)(2,1)}, u32[]{:S(2)}) copy-start(bf16[256,256]{1,0:T(8,128)(2,1)} %param.10) | copy-start | bytes 393220
  138.9 167.1 %reduce-scatter.3.cloned.1.call-start = ((), (), s32[]{:S(2)}) async-start(), calls=%async_computation.7 | async-start | bytes 1114112 | tf_op jit(solution)/shard_map/reduce_scatter | solution.py:121
  223.5 2.4 copy-start.3
Sparse Core Ops, SparseCore 0:
  142.4 81.0 reduce-scatter.4
  227.6 78.4 reduce-scatter.2
where the time goes:
time: 313 us
  blocking collectives  139 us (44%)
  waiting for transfers between devices  117 us (37%)
  starting transfers between devices  22.9 us (7%)
  matrix products  15.9 us (5%)
  between operations  14.3 us (5%)
    reduce_scatter x1, waiting for transfers between devices, on_device(): lax.psum_scatter(down_term, 'expert', scatter_dimension=0, tiled=True)  79.2 us
    psum x1, blocking collectives, on_device(): latent_grad, gate_grad = lax.psum((token_sums, gate_local), 'hidden')  66.5 us
    psum x1, blocking collectives, on_device(): cot_full = lax.psum(partial_cot, 'hidden')  62 us
    all_to_all x1, waiting for transfers between devices, on_device(): lax.all_to_all(latent_back, 'expert', split_axis=1, concat_axis=1, tiled=...  13.1 us
    all_to_all x1, blocking collectives, on_device(): lax.all_to_all(gate_send, 'expert', split_axis=1, concat_axis=1, tiled=True)  10.6 us
    all_to_all x1, waiting for transfers between devices, on_device(): lax.all_to_all(latent_rows.reshape(local_count, groups, capacity, latent_...  9.86 us
    all_to_all x1, waiting for transfers between devices, on_device(): lax.all_to_all(cot_rows.reshape(local_count, groups, capacity, latent_wid...  8.87 us
    all_to_all x1, starting transfers between devices, on_device(): lax.all_to_all(cot_rows.reshape(local_count, groups, capacity, latent_wid...  7.48 us
  transfers between devices with their start and end apart: 6, of which 5 were waited for; matrix products, arithmetic and copies ran while one was open for 4% of the time, Pallas kernels for 0%

commit v1 on v0

--- a/solution.py
+++ b/solution.py
@@ -44,7 +44,12 @@
     )
     gate_send = gate_slot.astype(jnp.bfloat16)
     dispatch_bf = hit_slot.astype(jnp.bfloat16).reshape(slot_total, tokens_here)
-    cot_full = lax.psum(partial_cot, "hidden")
+    n_parts = lax.axis_size("hidden")
+    cot_full = partial_cot
+    for dd in [
+        [(ii, ii ^ dev_i) for ii in range(n_parts)] for dev_i in (1, 2, 4, 8, 16) if dev_i < n_parts
+    ]:
+        cot_full = cot_full + lax.ppermute(cot_full, "hidden", dd)
     cot_rows = jnp.dot(
         dispatch_bf, cot_full.astype(jnp.bfloat16), preferred_element_type=jnp.float32
     ).astype(jnp.bfloat16)

time: 313 us -> 379 us (1.21)
  waiting for transfers between devices: 117 us -> 239 us
  blocking collectives: 139 us -> 71.8 us
  starting transfers between devices: 22.9 us -> 34.6 us
    ppermute x0 -> x4, waiting for transfers between devices: none -> 116 us  [on_device(): cot_full = cot_full + lax.ppermute(cot_full, 'hidden', dd)]
    psum x1 -> x0, blocking collectives: 62 us -> none  [on_device(): cot_full = lax.psum(partial_cot, 'hidden')]
    ppermute x0 -> x4, starting transfers between devices: none -> 11.8 us  [on_device(): cot_full = cot_full + lax.ppermute(cot_full, 'hidden', dd)]
    psum x1, blocking collectives: 66.5 us -> 61.3 us  [on_device(): latent_grad, gate_grad = lax.psum((token_sums, gate_local), 'hidden')]
  transfers between devices with their start and end apart: 6 -> 10, of which waited for: 5 -> 9; matrix products, arithmetic and copies ran while one was open for 4% -> 3% of each run, Pallas kernels for 0% -> 0%
where the time goes in v1:
time: 379 us
  waiting for transfers between devices  239 us (63%)
  blocking collectives  71.8 us (19%)
  starting transfers between devices  34.6 us (9%)
  matrix products  16 us (4%)
  between operations  14.3 us (4%)
    ppermute x4, waiting for transfers between devices, on_device(): cot_full = cot_full + lax.ppermute(cot_full, 'hidden', dd)  116 us
    reduce_scatter x1, waiting for transfers between devices, on_device(): lax.psum_scatter(down_term, 'expert', scatter_dimension=0, tiled=True)  79.2 us
    psum x1, blocking collectives, on_device(): latent_grad, gate_grad = lax.psum((token_sums, gate_local), 'hidden')  61.3 us
    all_to_all x1, waiting for transfers between devices, on_device(): lax.all_to_all(latent_back, 'expert', split_axis=1, concat_axis=1, tiled=...  15.6 us
    ppermute x4, starting transfers between devices, on_device(): cot_full = cot_full + lax.ppermute(cot_full, 'hidden', dd)  11.8 us
    all_to_all x1, waiting for transfers between devices, on_device(): lax.all_to_all(latent_rows.reshape(local_count, groups, capacity, latent_...  11 us
    all_to_all x1, waiting for transfers between devices, on_device(): lax.all_to_all(cot_rows.reshape(local_count, groups, capacity, latent_wid...  10.8 us
    all_to_all x1, blocking collectives, on_device(): lax.all_to_all(gate_send, 'expert', split_axis=1, concat_axis=1, tiled=True)  10.6 us
  transfers between devices with their start and end apart: 10, of which 9 were waited for; matrix products, arithmetic and copies ran while one was open for 3% of the time, Pallas kernels for 0%

profile of v1, /device:TPU:2, one launch (start us, length us, event | category | flops | bytes accessed | tf_op | source)
XLA Modules:
  0.0 378.6 jit_solution(8667762502702058519)
XLA Ops:
  7.2 1.5 fusion.22
  8.7 0.1 collective-permute-start
  8.8 2.6 collective-permute-done
  11.4 0.1 add.20
  11.6 2.0 collective-permute-start.1
  13.6 23.5 %collective-permute-done.1 = f32[256,1024]{1,0:T(8,128)S(1)} collective-permute-done((f32[256,1024]{1,0:T(8,128)S(1)}, f32[256,1024]{1,0:T(8,128)S(1)}, u32[]{:S(2)}, u32[]{:S(2)}) %collective-permute-start.1) | collective-permute-done | bytes 1048608 | tf_op jit(solution)/shard_map/ppermute | solution.py:52
  37.0 0.2 add.21
  37.2 3.4 collective-permute-start.2
  40.6 45.2 %collective-permute-done.2 = f32[256,1024]{1,0:T(8,128)S(1)} collective-permute-done((f32[256,1024]{1,0:T(8,128)S(1)}, f32[256,1024]{1,0:T(8,128)S(1)}, u32[]{:S(2)}, u32[]{:S(2)}) %collective-permute-start.2) | collective-permute-done | bytes 1048608 | tf_op jit(solution)/shard_map/ppermute | solution.py:52
  85.8 0.1 add.22
  86.0 6.3 %collective-permute-start.3 = (f32[256,1024]{1,0:T(8,128)S(1)}, f32[256,1024]{1,0:T(8,128)S(1)}, u32[]{:S(2)}, u32[]{:S(2)}) collective-permute-start(f32[256,1024]{1,0:T(8,128)S(1)} %add.22), channel_id=1, source_target_pairs={{0,8},{1,9},{2,10},{3,11},{4,12},{5,13},{6,14},{7,15},{8,0},{9,1},... | collective-permute-start | bytes 3145736 | tf_op jit(solution)/shard_map/ppermute | solution.py:52
  92.3 0.1 eq.79
  92.4 0.6 reduce-window.6
  93.0 0.2 slice_reduce_fusion
  93.2 0.1 bitcast_subtract_fusion
  93.3 0.1 fusion.8
  93.5 44.6 %collective-permute-done.3 = f32[256,1024]{1,0:T(8,128)S(1)} collective-permute-done((f32[256,1024]{1,0:T(8,128)S(1)}, f32[256,1024]{1,0:T(8,128)S(1)}, u32[]{:S(2)}, u32[]{:S(2)}) %collective-permute-start.3) | collective-permute-done | bytes 1048608 | tf_op jit(solution)/shard_map/ppermute | solution.py:52
  138.1 1.3 convolution_convert_fusion
  139.3 7.5 %all-to-all-start.2 = ((bf16[1,16,24,1024]{3,2,0,1:T(8,128)(2,1)}), bf16[1,16,24,1024]{3,2,0,1:T(8,128)(2,1)S(1)}, u32[]{:S(2)}, u32[]{:S(2)}) async-start(bf16[1,16,24,1024]{3,2,0,1:T(8,128)(2,1)} %bitcast.11), calls=%async_computation.2 | async-start | bytes 1572864 | tf_op jit(solution)/shard_map/all_to_all | solution.py:60
  146.8 1.3 convolution_convert_fusion.1
  148.1 10.8 %all-to-all-done.2 = bf16[1,16,24,1024]{3,2,0,1:T(8,128)(2,1)S(1)} async-done(((bf16[1,16,24,1024]{3,2,0,1:T(8,128)(2,1)}), bf16[1,16,24,1024]{3,2,0,1:T(8,128)(2,1)S(1)}, u32[]{:S(2)}, u32[]{:S(2)}) %all-to-all-start.2) | async-done | bytes 786464 | tf_op jit(solution)/shard_map/all_to_all | solution.py:60
  158.9 4.9 %all-to-all-start.1 = ((bf16[1,16,24,1024]{3,2,0,1:T(8,128)(2,1)}), bf16[1,16,24,1024]{3,2,0,1:T(8,128)(2,1)S(1)}, u32[]{:S(2)}, u32[]{:S(2)}) async-start(bf16[1,16,24,1024]{3,2,0,1:T(8,128)(2,1)} %bitcast.7), calls=%async_computation.1 | async-start | bytes 1572864 | tf_op jit(solution)/shard_map/all_to_all | solution.py:67
  163.8 0.4 fusion.10
  164.2 11.0 %all-to-all-done.1 = bf16[1,16,24,1024]{3,2,0,1:T(8,128)(2,1)S(1)} async-done(((bf16[1,16,24,1024]{3,2,0,1:T(8,128)(2,1)}), bf16[1,16,24,1024]{3,2,0,1:T(8,128)(2,1)S(1)}, u32[]{:S(2)}, u32[]{:S(2)}) %all-to-all-start.1) | async-done | bytes 786464 | tf_op jit(solution)/shard_map/all_to_all | solution.py:67
  175.2 0.5 fusion.16
  175.7 0.7 reshape.184
  176.4 4.7 %all-to-all-start.4 = ((f32[1,16,24]{2,0,1:T(1,128)}), f32[1,16,24]{2,0,1:T(1,128)S(1)}, u32[]{:S(2)}, u32[]{:S(2)}) async-start(f32[1,16,24]{2,0,1:T(1,128)} %reshape.184), calls=%async_computation.6 | async-start | bytes 16384 | tf_op jit(solution)/shard_map/all_to_all | solution.py:105
  181.1 6.2 %all-to-all-done.4 = f32[1,16,24]{2,0,1:T(1,128)S(1)} async-done(((f32[1,16,24]{2,0,1:T(1,128)}), f32[1,16,24]{2,0,1:T(1,128)S(1)}, u32[]{:S(2)}, u32[]{:S(2)}) %all-to-all-start.4) | async-done | bytes 1568 | tf_op jit(solution)/shard_map/all_to_all | solution.py:105
  187.3 0.2 select_reduce_fusion
  187.5 0.1 select_reduce_fusion.2
  187.6 0.2 select_reduce_fusion.1
  187.8 10.6 %all_to_all.25 = bf16[1,16,24]{2,0,1:T(2,128)(2,1)S(1)} all-to-all(bf16[1,16,24]{2,0,1:T(2,128)(2,1)S(1)} %copy.45), channel_id=1, replica_groups=mesh['expert'=16,'hidden'=16] {'expert'}, dimensions={1} | all-to-all | bytes 1536 | tf_op jit(solution)/shard_map/all_to_all | solution.py:74
  198.4 0.1 reshape.185
  198.5 0.1 copy.48
  198.7 1.5 convolution_bitcast_fusion
  200.2 5.7 %all-to-all-start.3 = ((f32[1,16,24,1024]{3,2,0,1:T(8,128)}), f32[1,16,24,1024]{3,2,0,1:T(8,128)}, u32[]{:S(2)}, u32[]{:S(2)}) async-start(f32[1,16,24,1024]{3,2,0,1:T(8,128)} %convolution_bitcast_fusion), calls=%async_computation.3 | async-start | bytes 3145728 | tf_op jit(solution)/shard_map/all_to_all | solution.py:104
  205.9 0.0 reduce-scatter.5.cloned.1.call-start
  206.0 1.3 fusion.23
  207.3 0.0 reduce-scatter.5.cloned.1.call-update
  207.3 0.0 reduce-scatter.3.cloned.1.call-start
  207.4 15.6 %all-to-all-done.3 = f32[1,16,24,1024]{3,2,0,1:T(8,128)} async-done(((f32[1,16,24,1024]{3,2,0,1:T(8,128)}), f32[1,16,24,1024]{3,2,0,1:T(8,128)}, u32[]{:S(2)}, u32[]{:S(2)}) %all-to-all-start.3) | async-done | bytes 1572896 | tf_op jit(solution)/shard_map/all_to_all | solution.py:104
  223.0 3.5 fusion.2
  226.5 61.3 %all-reduce.2 = (bf16[256,1024]{1,0:T(8,128)(2,1)S(1)}, f32[256,22]{0,1:T(8,128)}) all-reduce(f32[256,1024]{1,0:T(8,128)} %fusion.2, f32[256,22]{0,1:T(8,128)S(1)} %get-tuple-element.6), channel_id=1, replica_groups=mesh['expert'=16,'hidden'=16] {'hidden'}, use_global_device_ids=true, to_apply=%region_5.6 | all-reduce | flops 267776 | bytes 1617920 | tf_op jit(solution)/shard_map/psum | solution.py:116
  287.8 1.3 fusion.24
  289.1 1.2 convolution_bitcast_fusion.2
  290.3 1.2 convolution_bitcast_fusion.1
  291.5 1.0 convolution_convert_fusion.2
  292.5 79.2 %reduce-scatter.3.cloned.1.call-done = f32[64,256]{1,0:T(8,128)} async-done(((f32[1024,256]{1,0:T(8,128)}), f32[64,256]{1,0:T(8,128)}) %reduce-scatter.3.cloned.1.call-update) | async-done | bytes 65552 | tf_op jit(solution)/shard_map/reduce_scatter | solution.py:126
  (31 shorter events, 0.3 us)
Async XLA Ops:
  7.2 139.7 %copy-start = (bf16[256,1024]{1,0:T(8,128)(2,1)S(1)}, bf16[256,1024]{1,0:T(8,128)(2,1)}, u32[]{:S(2)}) copy-start(bf16[256,1024]{1,0:T(8,128)(2,1)} %param.12) | copy-start | bytes 1572868
  8.7 2.7 collective-permute-start
  11.6 25.5 %collective-permute-start.1 = (f32[256,1024]{1,0:T(8,128)S(1)}, f32[256,1024]{1,0:T(8,128)S(1)}, u32[]{:S(2)}, u32[]{:S(2)}) collective-permute-start(f32[256,1024]{1,0:T(8,128)S(1)} %add.20), channel_id=1, source_target_pairs={{0,2},{1,3},{2,0},{3,1},{4,6},{5,7},{6,4},{7,5},{8,10},{9,11},{10,... | collective-permute-start | bytes 3145736 | tf_op jit(solution)/shard_map/ppermute | solution.py:52
  37.2 55.2 %copy-start.7 = (s32[256,22]{0,1:T(8,128)S(1)}, s32[256,22]{0,1:T(8,128)}, u32[]{:S(2)}) copy-start(s32[256,22]{0,1:T(8,128)} %param.14) | copy-start | bytes 67588
  37.2 48.6 %collective-permute-start.2 = (f32[256,1024]{1,0:T(8,128)S(1)}, f32[256,1024]{1,0:T(8,128)S(1)}, u32[]{:S(2)}, u32[]{:S(2)}) collective-permute-start(f32[256,1024]{1,0:T(8,128)S(1)} %add.21), channel_id=1, source_target_pairs={{0,4},{1,5},{2,6},{3,7},{4,0},{5,1},{6,2},{7,3},{8,12},{9,13},{10,... | collective-permute-start | bytes 3145736 | tf_op jit(solution)/shard_map/ppermute | solution.py:52
  86.0 52.1 %collective-permute-start.3 = (f32[256,1024]{1,0:T(8,128)S(1)}, f32[256,1024]{1,0:T(8,128)S(1)}, u32[]{:S(2)}, u32[]{:S(2)}) collective-permute-start(f32[256,1024]{1,0:T(8,128)S(1)} %add.22), channel_id=1, source_target_pairs={{0,8},{1,9},{2,10},{3,11},{4,12},{5,13},{6,14},{7,15},{8,0},{9,1},... | collective-permute-start | bytes 3145736 | tf_op jit(solution)/shard_map/ppermute | solution.py:52
  139.3 19.6 %all-to-all-start.2 = ((bf16[1,16,24,1024]{3,2,0,1:T(8,128)(2,1)}), bf16[1,16,24,1024]{3,2,0,1:T(8,128)(2,1)S(1)}, u32[]{:S(2)}, u32[]{:S(2)}) async-start(bf16[1,16,24,1024]{3,2,0,1:T(8,128)(2,1)} %bitcast.11), calls=%async_computation.2 | async-start | bytes 1572864 | tf_op jit(solution)/shard_map/all_to_all | solution.py:60
  146.8 17.0 %copy-start.5 = (bf16[1,168,1024]{2,1,0:T(8,128)(2,1)S(1)}, bf16[1,168,1024]{2,1,0:T(8,128)(2,1)}, u32[]{:S(2)}) copy-start(bf16[1,168,1024]{2,1,0:T(8,128)(2,1)} %param.19) | copy-start | bytes 1032196
  148.1 27.1 %copy-start.1 = (bf16[1,1024,168]{1,2,0:T(8,128)(2,1)S(1)}, bf16[1,1024,168]{1,2,0:T(8,128)(2,1)}, u32[]{:S(2)}) copy-start(bf16[1,1024,168]{1,2,0:T(8,128)(2,1)} %param.18) | copy-start | bytes 1032196
  158.9 16.3 %all-to-all-start.1 = ((bf16[1,16,24,1024]{3,2,0,1:T(8,128)(2,1)}), bf16[1,16,24,1024]{3,2,0,1:T(8,128)(2,1)S(1)}, u32[]{:S(2)}, u32[]{:S(2)}) async-start(bf16[1,16,24,1024]{3,2,0,1:T(8,128)(2,1)} %bitcast.7), calls=%async_computation.1 | async-start | bytes 1572864 | tf_op jit(solution)/shard_map/all_to_all | solution.py:67
  163.8 17.3 %copy-start.8 = (bf16[256,22]{0,1:T(8,128)(2,1)S(1)}, bf16[256,22]{0,1:T(8,128)(2,1)}, u32[]{:S(2)}) copy-start(bf16[256,22]{0,1:T(8,128)(2,1)} %param.15) | copy-start | bytes 33796
  176.4 10.9 %all-to-all-start.4 = ((f32[1,16,24]{2,0,1:T(1,128)}), f32[1,16,24]{2,0,1:T(1,128)S(1)}, u32[]{:S(2)}, u32[]{:S(2)}) async-start(f32[1,16,24]{2,0,1:T(1,128)} %reshape.184), calls=%async_computation.6 | async-start | bytes 16384 | tf_op jit(solution)/shard_map/all_to_all | solution.py:105
  200.2 5.8 %copy-start.2 = (bf16[256,1024]{1,0:T(8,128)(2,1)S(1)}, bf16[256,1024]{1,0:T(8,128)(2,1)}, u32[]{:S(2)}) copy-start(bf16[256,1024]{1,0:T(8,128)(2,1)} %param.13) | copy-start | bytes 1572868
  200.2 5.8 %copy-start.4 = (bf16[256,256]{1,0:T(8,128)(2,1)S(1)}, bf16[256,256]{1,0:T(8,128)(2,1)}, u32[]{:S(2)}) copy-start(bf16[256,256]{1,0:T(8,128)(2,1)} %param.11) | copy-start | bytes 393220
  200.2 22.8 %all-to-all-start.3 = ((f32[1,16,24,1024]{3,2,0,1:T(8,128)}), f32[1,16,24,1024]{3,2,0,1:T(8,128)}, u32[]{:S(2)}, u32[]{:S(2)}) async-start(f32[1,16,24,1024]{3,2,0,1:T(8,128)} %convolution_bitcast_fusion), calls=%async_computation.3 | async-start | bytes 3145728 | tf_op jit(solution)/shard_map/all_to_all | solution.py:104
  205.9 86.6 %reduce-scatter.5.cloned.1.call-start = ((), (), s32[]{:S(2)}) async-start(), calls=%async_computation.8 | async-start | bytes 1114112 | tf_op jit(solution)/shard_map/reduce_scatter | solution.py:127
  207.3 80.4 %copy-start.6 = (bf16[256,256]{1,0:T(8,128)(2,1)S(1)}, bf16[256,256]{1,0:T(8,128)(2,1)}, u32[]{:S(2)}) copy-start(bf16[256,256]{1,0:T(8,128)(2,1)} %param.10) | copy-start | bytes 393220
  207.3 164.4 %reduce-scatter.3.cloned.1.call-start = ((), (), s32[]{:S(2)}) async-start(), calls=%async_computation.7 | async-start | bytes 1114112 | tf_op jit(solution)/shard_map/reduce_scatter | solution.py:126
  289.1 2.4 copy-start.3
Sparse Core Ops, SparseCore 0:
  210.8 78.3 reduce-scatter.4
  293.3 78.4 reduce-scatter.2
